TPU v7x, 256 devices: a whole 4x4x8 slice. The times are simulated.
256 devices in a mesh: wide: 32 (over x, z_hi, core), narrow: 8 (over y, z_lo).
Axes of the slice: x: 4, y: 4, z: 8 (z_hi: 4, z_lo: 2; z = z_hi * 2 + z_lo), core: 2. Of those that a mesh axis runs over, the one named last changes fastest.
Arguments:
- state_real: float32 [8, 32, 4096, 128], P('narrow', 'wide'), may hold values from -6 to 6
- state_imag: float32 [8, 32, 4096, 128], P('narrow', 'wide'), may hold values from -6 to 6
- gates: float32 [3, 2, 128, 128], replicated, may hold values from -0.375 to 0.375
- gate_orders: int32 [3, 7], replicated, may hold values from 0 to 6, each once within a row
- phase_masks: int32 [8, 2], replicated, may hold values from 1 to 67108864, as said below
- phase_angles: float32 [8], replicated, may hold values from -3.140625 to 3.140625
Outputs:
- out_real: float32 [8, 32, 4096, 128], P('narrow', 'wide')
- out_imag: float32 [8, 32, 4096, 128], P('narrow', 'wide')
Inputs may be any that keep to these rules, and one draw needn't show every extreme that they name: `phase_masks`: each entry is 2**q for one qubit q of the whole index of 134217728 amplitudes; the two entries of a row differ.
All inputs are finite; a program needn't handle non-finite values.
Results may differ from a plain program's by a relative error of at most 0.0003.
Values sent between devices are 32-bit elements; how exact they have to be, the bound alone decides.
No kernel may reach another device: no remote copies, remote signals or barrier semaphores. Data moves between devices by JAX's collectives and lax.ppermute only.
A program may use at most 64 MiB of HBM per device.

v0:
```python
import jax
import jax.numpy as jnp
from jax import lax
from jax.sharding import PartitionSpec as P

precise = lax.Precision.HIGHEST


def partner(block, axis, stride):
    count = lax.axis_size(axis)
    route = []
    for low in range(count):
        high = low | 1 << stride
        if high != low and high < count:
            route += [(low, high), (high, low)]
    return lax.ppermute(block, axis, route)


def ordered_gate(gate_pair, order_row):
    count = order_row.shape[0]
    states = jnp.arange(2**count, dtype=jnp.int32)
    places = jnp.arange(count, dtype=jnp.int32)
    digits = states[:, None] >> places[None, :] & 1
    mapped = jnp.sum(digits << order_row[None, :], axis=1)
    permute = (mapped[:, None] == states[None, :]).astype(jnp.float32)
    real_gate = jnp.dot(
        jnp.dot(permute, gate_pair[0], precision=precise), permute.T, precision=precise
    )
    imag_gate = jnp.dot(
        jnp.dot(permute, gate_pair[1], precision=precise), permute.T, precision=precise
    )
    return (real_gate, imag_gate)


def mixing(gate_real, gate_imag, real_part, imag_part):
    out_real = jnp.dot(gate_real, real_part, precision=precise) - jnp.dot(
        gate_imag, imag_part, precision=precise
    )
    out_imag = jnp.dot(gate_real, imag_part, precision=precise) + jnp.dot(
        gate_imag, real_part, precision=precise
    )
    return (out_real, out_imag)


def phase_turn(real_part, imag_part, flat, phase_masks, phase_angles):
    angle_sum = jnp.zeros(real_part.shape, jnp.float32)
    for which in range(phase_masks.shape[0]):
        both = (flat & phase_masks[which, 0] != 0) & (flat & phase_masks[which, 1] != 0)
        angle_sum = angle_sum + jnp.where(both, phase_angles[which], 0.0)
    cosine = jnp.cos(angle_sum)
    sine = jnp.sin(angle_sum)
    return (real_part * cosine - imag_part * sine, real_part * sine + imag_part * cosine)


def global_exchange(real_part, imag_part, gate_real, gate_imag, devices, outward, inward):
    row_count, columns = real_part.shape
    gate_size = gate_real.shape[0]
    blocks = gate_size // devices
    stride = row_count // blocks
    moved_real, moved_imag = outward(
        (
            real_part.reshape(1, blocks, stride, columns),
            imag_part.reshape(1, blocks, stride, columns),
        )
    )
    mixed_real, mixed_imag = mixing(
        gate_real, gate_imag, moved_real.reshape(gate_size, -1), moved_imag.reshape(gate_size, -1)
    )
    back_real, back_imag = inward(
        (mixed_real.reshape(moved_real.shape), mixed_imag.reshape(moved_imag.shape))
    )
    return (back_real.reshape(row_count, columns), back_imag.reshape(row_count, columns))


def swap_half(pieces, which_bit, own_index, sender):
    real_part, imag_part = pieces
    blocks, devices, stride, columns = real_part.shape
    split_shape = (blocks, devices >> which_bit + 1, 2, 1 << which_bit, stride, columns)
    own_bit = own_index >> which_bit & 1
    split_real = real_part.reshape(split_shape)
    split_imag = imag_part.reshape(split_shape)
    outgoing = (
        lax.dynamic_slice_in_dim(split_real, 1 - own_bit, 1, 2),
        lax.dynamic_slice_in_dim(split_imag, 1 - own_bit, 1, 2),
    )
    gotten = sender(outgoing, which_bit)
    result = []
    for kept_whole, arrived in ((split_real, gotten[0]), (split_imag, gotten[1])):
        kept_half = lax.dynamic_slice_in_dim(kept_whole, own_bit, 1, 2)
        joined = jnp.where(
            own_bit == 0,
            jnp.concatenate([kept_half, arrived], axis=2),
            jnp.concatenate([arrived, kept_half], axis=2),
        )
        result.append(joined.reshape(real_part.shape))
    return (result[0], result[1])


def global_halves(real_part, imag_part, gate_real, gate_imag, devices, own_index, sender):
    row_count, columns = real_part.shape
    gate_size = gate_real.shape[0]
    blocks = gate_size // devices
    stride = row_count // blocks
    local_shape = (blocks, devices, stride // devices, columns)
    pieces = (real_part.reshape(local_shape), imag_part.reshape(local_shape))
    levels = devices.bit_length() - 1
    for which_bit in range(levels):
        pieces = swap_half(pieces, which_bit, own_index, sender)
    turned_real = (
        gate_real.reshape(devices, blocks, devices, blocks)
        .transpose(1, 0, 3, 2)
        .reshape(gate_size, gate_size)
    )
    turned_imag = (
        gate_imag.reshape(devices, blocks, devices, blocks)
        .transpose(1, 0, 3, 2)
        .reshape(gate_size, gate_size)
    )
    mixed_real, mixed_imag = mixing(
        turned_real, turned_imag, pieces[0].reshape(gate_size, -1), pieces[1].reshape(gate_size, -1)
    )
    pieces = (mixed_real.reshape(local_shape), mixed_imag.reshape(local_shape))
    for which_bit in range(levels):
        pieces = swap_half(pieces, which_bit, own_index, sender)
    return (pieces[0].reshape(row_count, columns), pieces[1].reshape(row_count, columns))


def body(state_real, state_imag, gates, gate_orders, phase_masks, phase_angles):
    real_part = state_real[0, 0]
    imag_part = state_imag[0, 0]
    row_count, columns = real_part.shape
    first_gate = ordered_gate(gates[0], gate_orders[0])
    second_gate = ordered_gate(gates[1], gate_orders[1])
    third_gate = ordered_gate(gates[2], gate_orders[2])
    new_real = jnp.dot(real_part, first_gate[0].T, precision=precise) - jnp.dot(
        imag_part, first_gate[1].T, precision=precise
    )
    new_imag = jnp.dot(imag_part, first_gate[0].T, precision=precise) + jnp.dot(
        real_part, first_gate[1].T, precision=precise
    )
    wide_count = lax.axis_size("wide")
    narrow_count = lax.axis_size("narrow")
    wide_index = lax.axis_index("wide")
    narrow_index = lax.axis_index("narrow")
    offset = (narrow_index * wide_count + wide_index) * (row_count * columns)
    flat = (
        offset
        + jnp.arange(row_count, dtype=jnp.int32)[:, None] * columns
        + jnp.arange(columns, dtype=jnp.int32)[None, :]
    )
    turned_real, turned_imag = phase_turn(new_real, new_imag, flat, phase_masks, phase_angles)
    middle_real, middle_imag = global_exchange(
        turned_real,
        turned_imag,
        second_gate[0],
        second_gate[1],
        wide_count,
        lambda pieces: (
            lax.all_to_all(pieces[0], "wide", split_axis=2, concat_axis=0, tiled=True),
            lax.all_to_all(pieces[1], "wide", split_axis=2, concat_axis=0, tiled=True),
        ),
        lambda pieces: (
            lax.all_to_all(pieces[0], "wide", split_axis=0, concat_axis=2, tiled=True),
            lax.all_to_all(pieces[1], "wide", split_axis=0, concat_axis=2, tiled=True),
        ),
    )
    final_real, final_imag = global_halves(
        middle_real,
        middle_imag,
        third_gate[0],
        third_gate[1],
        narrow_count,
        narrow_index,
        lambda pieces, which_bit: partner((pieces[0], pieces[1]), "narrow", which_bit),
    )
    return (final_real[None, None], final_imag[None, None])


def solution(mesh):
    placed = (P("narrow", "wide", None, None), P("narrow", "wide", None, None), P(), P(), P(), P())
    return jax.shard_map(
        body,
        mesh=mesh,
        in_specs=placed,
        out_specs=(P("narrow", "wide", None, None), P("narrow", "wide", None, None)),
        check_vma=False,
    )
```

profile of v0, /device:TPU:2, one launch (start us, length us, event | category | flops | bytes accessed | tf_op | source)
XLA Modules:
  0.0 565.0 jit_solution(16842037079720946697)
XLA Ops:
  7.9 3.5 fusion.14
  15.4 30.1 %multiply_subtract_fusion = (f32[4096,128]{0,1:T(8,128)}, f32[4096,128]{0,1:T(8,128)S(1)}) fusion(f32[4096,128]{0,1:T(8,128)S(1)} %fusion.1, f32[]{:T(128)} %bitcast.34, s32[]{:T(128)} %bitcast.33, s32[]{:T(128)} %bitcast.32, f32[]{:T(128)} %bitcast.31, s32[]{:T(128)} %bitcast.30, s32[]{:T(128)} %bitcast.29, f32[]{:T(128)} %bitcast.28, s32[]{:T(128)} %bitcast.27, ...), kind=kOutput, calls=%fused_computation.39 | convolution fusion | flops 836763648 | bytes 10567776 | tf_op jit(solution)/shard_map/dot_general | solution.py:138
  45.5 26.3 %multiply_add_fusion = f32[4096,128]{0,1:T(8,128)S(1)} fusion(f32[4096,128]{0,1:T(8,128)S(1)} %get-tuple-element.54, f32[4096,128]{0,1:T(8,128)S(1)} %fusion.1, f32[]{:T(128)} %bitcast.34, s32[]{:T(128)} %bitcast.33, s32[]{:T(128)} %bitcast.32, f32[]{:T(128)} %bitcast.31, s32[]{:T(128)} %bitcast.30, s32[]{:T(128)} %bitcast.29, f32[]{:T(128)} %bitcast.28, ...), kind=kLoop, calls=%fused_computation.38 | loop fusion | flops 30932992 | bytes 6307936 | tf_op jit(solution)/shard_map/add | solution.py:52
  74.3 3.9 copy.46
  78.2 11.6 %all-to-all-start.1 = ((f32[1,4,1024,128]{3,1,0,2:T(4,128)}), f32[1,4,1024,128]{3,1,0,2:T(4,128)S(1)}, u32[]{:S(2)}, u32[]{:S(2)}) async-start(f32[1,4,1024,128]{3,1,0,2:T(4,128)} %copy.46), calls=%async_computation.1 | async-start | bytes 4194304 | tf_op jit(solution)/shard_map/all_to_all | solution.py:160
  89.8 3.6 reshape.422
  93.5 3.9 copy.43
  97.4 39.9 %all-to-all-done.1 = f32[1,4,1024,128]{3,1,0,2:T(4,128)S(1)} async-done(((f32[1,4,1024,128]{3,1,0,2:T(4,128)}), f32[1,4,1024,128]{3,1,0,2:T(4,128)S(1)}, u32[]{:S(2)}, u32[]{:S(2)}) %all-to-all-start.1) | async-done | bytes 2097184 | tf_op jit(solution)/shard_map/all_to_all | solution.py:160
  137.2 8.6 %all-to-all-start = ((f32[1,4,1024,128]{3,1,0,2:T(4,128)}), f32[1,4,1024,128]{3,1,0,2:T(4,128)}, u32[]{:S(2)}, u32[]{:S(2)}) async-start(f32[1,4,1024,128]{3,1,0,2:T(4,128)} %copy.43), calls=%async_computation | async-start | bytes 4194304 | tf_op jit(solution)/shard_map/all_to_all | solution.py:159
  147.3 39.6 %all-to-all-done = f32[1,4,1024,128]{3,1,0,2:T(4,128)} async-done(((f32[1,4,1024,128]{3,1,0,2:T(4,128)}), f32[1,4,1024,128]{3,1,0,2:T(4,128)}, u32[]{:S(2)}, u32[]{:S(2)}) %all-to-all-start) | async-done | bytes 2097184 | tf_op jit(solution)/shard_map/all_to_all | solution.py:159
  191.9 3.0 fusion.36
  196.7 15.0 %all-to-all-start.2 = ((f32[32,4,32,128]{3,2,1,0:T(8,128)}), f32[32,4,32,128]{3,2,1,0:T(8,128)}, u32[]{:S(2)}, u32[]{:S(2)}) async-start(f32[32,4,32,128]{3,2,1,0:T(8,128)} %bitcast.200), calls=%async_computation.2 | async-start | bytes 4194304 | tf_op jit(solution)/shard_map/all_to_all | solution.py:163
  214.7 3.1 fusion.39
  219.5 34.7 %all-to-all-done.2 = f32[32,4,32,128]{3,2,1,0:T(8,128)} async-done(((f32[32,4,32,128]{3,2,1,0:T(8,128)}), f32[32,4,32,128]{3,2,1,0:T(8,128)}, u32[]{:S(2)}, u32[]{:S(2)}) %all-to-all-start.2) | async-done | bytes 2097184 | tf_op jit(solution)/shard_map/all_to_all | solution.py:163
  254.2 13.6 %all-to-all-start.3 = ((f32[32,4,32,128]{3,2,1,0:T(8,128)}), f32[32,4,32,128]{3,2,1,0:T(8,128)}, u32[]{:S(2)}, u32[]{:S(2)}) async-start(f32[32,4,32,128]{3,2,1,0:T(8,128)} %bitcast.199), calls=%async_computation.3 | async-start | bytes 4194304 | tf_op jit(solution)/shard_map/all_to_all | solution.py:164
  273.7 36.9 %all-to-all-done.3 = f32[32,4,32,128]{3,2,1,0:T(8,128)} async-done(((f32[32,4,32,128]{3,2,1,0:T(8,128)}), f32[32,4,32,128]{3,2,1,0:T(8,128)}, u32[]{:S(2)}, u32[]{:S(2)}) %all-to-all-start.3) | async-done | bytes 2097184 | tf_op jit(solution)/shard_map/all_to_all | solution.py:164
  313.7 8.5 %collective-permute-start.3 = (f32[16,4,1,1,32,128]{5,4,2,1,0,3:T(8,128)}, f32[16,4,1,1,32,128]{5,4,2,1,0,3:T(8,128)}, u32[]{:S(2)}, u32[]{:S(2)}) collective-permute-start(f32[16,4,1,1,32,128]{5,4,2,1,0,3:T(8,128)} %get-tuple-element.19), channel_id=1, source_target_pairs={{0,1},{1,0},{2,3},{3,2},{4,5},{5,4},{6,7},{7,6},{8,9},{9,8},{10,11... | collective-permute-start | bytes 3145736 | tf_op jit(solution)/shard_map/ppermute | solution.py:16
  322.2 16.6 %collective-permute-done = f32[16,4,1,1,32,128]{5,4,2,1,0,3:T(8,128)} collective-permute-done((f32[16,4,1,1,32,128]{5,4,2,1,0,3:T(8,128)}, f32[16,4,1,1,32,128]{5,4,2,1,0,3:T(8,128)}, u32[]{:S(2)}, u32[]{:S(2)}) %collective-permute-start) | collective-permute-done | bytes 1048608 | tf_op jit(solution)/shard_map/ppermute | solution.py:16
  345.7 15.5 %collective-permute-done.3 = f32[16,4,1,1,32,128]{5,4,2,1,0,3:T(8,128)} collective-permute-done((f32[16,4,1,1,32,128]{5,4,2,1,0,3:T(8,128)}, f32[16,4,1,1,32,128]{5,4,2,1,0,3:T(8,128)}, u32[]{:S(2)}, u32[]{:S(2)}) %collective-permute-start.3) | collective-permute-done | bytes 1048608 | tf_op jit(solution)/shard_map/ppermute | solution.py:16
  366.4 3.6 collective-permute-done.1
  369.9 3.0 maximum_select_fusion.1
  376.7 15.7 %collective-permute-done.4 = f32[16,2,1,2,32,128]{5,4,3,2,1,0:T(8,128)} collective-permute-done((f32[16,2,1,2,32,128]{5,4,3,2,1,0:T(8,128)}, f32[16,2,1,2,32,128]{5,4,3,2,1,0:T(8,128)}, u32[]{:S(2)}, u32[]{:S(2)}) %collective-permute-start.4) | collective-permute-done | bytes 1048608 | tf_op jit(solution)/shard_map/ppermute | solution.py:16
  400.5 15.2 %collective-permute-done.2 = f32[16,1,1,4,32,128]{5,4,3,2,0,1:T(8,128)} collective-permute-done((f32[16,1,1,4,32,128]{5,4,3,2,0,1:T(8,128)}, f32[16,1,1,4,32,128]{5,4,3,2,0,1:T(8,128)}, u32[]{:S(2)}, u32[]{:S(2)}) %collective-permute-start.2) | collective-permute-done | bytes 1048608 | tf_op jit(solution)/shard_map/ppermute | solution.py:16
  417.8 3.0 fusion.6
  420.8 16.4 %collective-permute-done.5 = f32[16,1,1,4,32,128]{5,4,3,2,0,1:T(8,128)} collective-permute-done((f32[16,1,1,4,32,128]{5,4,3,2,0,1:T(8,128)}, f32[16,1,1,4,32,128]{5,4,3,2,0,1:T(8,128)}, u32[]{:S(2)}, u32[]{:S(2)}) %collective-permute-start.5) | collective-permute-done | bytes 1048608 | tf_op jit(solution)/shard_map/ppermute | solution.py:16
  442.1 3.0 fusion.42
  446.3 3.0 fusion.45
  451.7 20.3 %collective-permute-done.6 = f32[16,4,1,1,32,128]{5,4,2,1,0,3:T(8,128)S(1)} collective-permute-done((f32[16,4,1,1,32,128]{5,4,2,1,0,3:T(8,128)S(1)}, f32[16,4,1,1,32,128]{5,4,2,1,0,3:T(8,128)S(1)}, u32[]{:S(2)}, u32[]{:S(2)}) %collective-permute-start.6) | collective-permute-done | bytes 1048608 | tf_op jit(solution)/shard_map/ppermute | solution.py:16
  472.7 20.0 %collective-permute-done.9 = f32[16,4,1,1,32,128]{5,4,2,1,0,3:T(8,128)S(1)} collective-permute-done((f32[16,4,1,1,32,128]{5,4,2,1,0,3:T(8,128)S(1)}, f32[16,4,1,1,32,128]{5,4,2,1,0,3:T(8,128)S(1)}, u32[]{:S(2)}, u32[]{:S(2)}) %collective-permute-start.9) | collective-permute-done | bytes 1048608 | tf_op jit(solution)/shard_map/ppermute | solution.py:16
  496.8 22.5 %collective-permute-done.10 = f32[16,2,1,2,32,128]{5,4,3,2,1,0:T(8,128)S(1)} collective-permute-done((f32[16,2,1,2,32,128]{5,4,3,2,1,0:T(8,128)S(1)}, f32[16,2,1,2,32,128]{5,4,3,2,1,0:T(8,128)S(1)}, u32[]{:S(2)}, u32[]{:S(2)}) %collective-permute-start.10) | collective-permute-done | bytes 1048608 | tf_op jit(solution)/shard_map/ppermute | solution.py:16
  521.9 20.8 %collective-permute-done.8 = f32[16,1,1,4,32,128]{5,4,3,2,0,1:T(8,128)S(1)} collective-permute-done((f32[16,1,1,4,32,128]{5,4,3,2,0,1:T(8,128)S(1)}, f32[16,1,1,4,32,128]{5,4,3,2,0,1:T(8,128)S(1)}, u32[]{:S(2)}, u32[]{:S(2)}) %collective-permute-start.8) | collective-permute-done | bytes 1048608 | tf_op jit(solution)/shard_map/ppermute | solution.py:16
  544.3 18.1 %collective-permute-done.11 = f32[16,1,1,4,32,128]{5,4,3,2,0,1:T(8,128)S(1)} collective-permute-done((f32[16,1,1,4,32,128]{5,4,3,2,0,1:T(8,128)S(1)}, f32[16,1,1,4,32,128]{5,4,3,2,0,1:T(8,128)S(1)}, u32[]{:S(2)}, u32[]{:S(2)}) %collective-permute-start.11) | collective-permute-done | bytes 1048608 | tf_op jit(solution)/shard_map/ppermute | solution.py:16
  (91 shorter events, 80.8 us)
Async XLA Ops:
  0.6 10.8 %copy-start = (f32[1,1,4096,128]{3,2,1,0:T(8,128)S(1)}, f32[1,1,4096,128]{3,2,1,0:T(8,128)}, u32[]{:S(2)}) copy-start(f32[1,1,4096,128]{3,2,1,0:T(8,128)} %param.6) | copy-start | bytes 6291460
  11.4 2.0 copy-start.4
  78.2 59.0 %all-to-all-start.1 = ((f32[1,4,1024,128]{3,1,0,2:T(4,128)}), f32[1,4,1024,128]{3,1,0,2:T(4,128)S(1)}, u32[]{:S(2)}, u32[]{:S(2)}) async-start(f32[1,4,1024,128]{3,1,0,2:T(4,128)} %copy.46), calls=%async_computation.1 | async-start | bytes 4194304 | tf_op jit(solution)/shard_map/all_to_all | solution.py:160
  97.4 48.5 %copy-start.7 = (f32[3,2,128,128]{3,2,1,0:T(8,128)S(1)}, f32[3,2,128,128]{3,2,1,0:T(8,128)}, u32[]{:S(2)}) copy-start(f32[3,2,128,128]{3,2,1,0:T(8,128)} %param.8) | copy-start | bytes 1179652
  137.2 49.7 %all-to-all-start = ((f32[1,4,1024,128]{3,1,0,2:T(4,128)}), f32[1,4,1024,128]{3,1,0,2:T(4,128)}, u32[]{:S(2)}, u32[]{:S(2)}) async-start(f32[1,4,1024,128]{3,1,0,2:T(4,128)} %copy.43), calls=%async_computation | async-start | bytes 4194304 | tf_op jit(solution)/shard_map/all_to_all | solution.py:159
  188.9 3.0 copy-start.2
  196.7 57.5 %all-to-all-start.2 = ((f32[32,4,32,128]{3,2,1,0:T(8,128)}), f32[32,4,32,128]{3,2,1,0:T(8,128)}, u32[]{:S(2)}, u32[]{:S(2)}) async-start(f32[32,4,32,128]{3,2,1,0:T(8,128)} %bitcast.200), calls=%async_computation.2 | async-start | bytes 4194304 | tf_op jit(solution)/shard_map/all_to_all | solution.py:163
  211.6 3.0 copy-start.3
  254.2 56.5 %all-to-all-start.3 = ((f32[32,4,32,128]{3,2,1,0:T(8,128)}), f32[32,4,32,128]{3,2,1,0:T(8,128)}, u32[]{:S(2)}, u32[]{:S(2)}) async-start(f32[32,4,32,128]{3,2,1,0:T(8,128)} %bitcast.199), calls=%async_computation.3 | async-start | bytes 4194304 | tf_op jit(solution)/shard_map/all_to_all | solution.py:164
  271.2 67.6 %collective-permute-start = (f32[16,4,1,1,32,128]{5,4,2,1,0,3:T(8,128)}, f32[16,4,1,1,32,128]{5,4,2,1,0,3:T(8,128)}, u32[]{:S(2)}, u32[]{:S(2)}) collective-permute-start(f32[16,4,1,1,32,128]{5,4,2,1,0,3:T(8,128)} %get-tuple-element.25), channel_id=1, source_target_pairs={{0,1},{1,0},{2,3},{3,2},{4,5},{5,4},{6,7},{7,6},{8,9},{9,8},{10,11... | collective-permute-start | bytes 3145736 | tf_op jit(solution)/shard_map/ppermute | solution.py:16
  313.7 47.5 %collective-permute-start.3 = (f32[16,4,1,1,32,128]{5,4,2,1,0,3:T(8,128)}, f32[16,4,1,1,32,128]{5,4,2,1,0,3:T(8,128)}, u32[]{:S(2)}, u32[]{:S(2)}) collective-permute-start(f32[16,4,1,1,32,128]{5,4,2,1,0,3:T(8,128)} %get-tuple-element.19), channel_id=1, source_target_pairs={{0,1},{1,0},{2,3},{3,2},{4,5},{5,4},{6,7},{7,6},{8,9},{9,8},{10,11... | collective-permute-start | bytes 3145736 | tf_op jit(solution)/shard_map/ppermute | solution.py:16
  343.2 26.7 %collective-permute-start.1 = (f32[16,2,1,2,32,128]{5,4,3,2,1,0:T(8,128)}, f32[16,2,1,2,32,128]{5,4,3,2,1,0:T(8,128)}, u32[]{:S(2)}, u32[]{:S(2)}) collective-permute-start(f32[16,2,1,2,32,128]{5,4,3,2,1,0:T(8,128)} %get-tuple-element.23), channel_id=1, source_target_pairs={{0,2},{2,0},{1,3},{3,1},{4,6},{6,4},{5,7},{7,5},{8,10},{10,8},{9,1... | collective-permute-start | bytes 3145736 | tf_op jit(solution)/shard_map/ppermute | solution.py:16
  364.3 28.1 %collective-permute-start.4 = (f32[16,2,1,2,32,128]{5,4,3,2,1,0:T(8,128)}, f32[16,2,1,2,32,128]{5,4,3,2,1,0:T(8,128)}, u32[]{:S(2)}, u32[]{:S(2)}) collective-permute-start(f32[16,2,1,2,32,128]{5,4,3,2,1,0:T(8,128)} %get-tuple-element.17), channel_id=1, source_target_pairs={{0,2},{2,0},{1,3},{3,1},{4,6},{6,4},{5,7},{7,5},{8,10},{10,8},{9,1... | collective-permute-start | bytes 3145736 | tf_op jit(solution)/shard_map/ppermute | solution.py:16
  374.6 41.1 %collective-permute-start.2 = (f32[16,1,1,4,32,128]{5,4,3,2,0,1:T(8,128)}, f32[16,1,1,4,32,128]{5,4,3,2,0,1:T(8,128)}, u32[]{:S(2)}, u32[]{:S(2)}) collective-permute-start(f32[16,1,1,4,32,128]{5,4,3,2,0,1:T(8,128)} %get-tuple-element.21), channel_id=1, source_target_pairs={{0,4},{4,0},{1,5},{5,1},{2,6},{6,2},{3,7},{7,3},{8,12},{12,8},{9,1... | collective-permute-start | bytes 3145736 | tf_op jit(solution)/shard_map/ppermute | solution.py:16
  396.0 41.2 %collective-permute-start.5 = (f32[16,1,1,4,32,128]{5,4,3,2,0,1:T(8,128)}, f32[16,1,1,4,32,128]{5,4,3,2,0,1:T(8,128)}, u32[]{:S(2)}, u32[]{:S(2)}) collective-permute-start(f32[16,1,1,4,32,128]{5,4,3,2,0,1:T(8,128)} %get-tuple-element.15), channel_id=1, source_target_pairs={{0,4},{4,0},{1,5},{5,1},{2,6},{6,2},{3,7},{7,3},{8,12},{12,8},{9,1... | collective-permute-start | bytes 3145736 | tf_op jit(solution)/shard_map/ppermute | solution.py:16
  399.1 16.6 %copy-start.5 = (f32[16,1,1,4,32,128]{5,4,3,2,0,1:T(8,128)S(1)}, f32[16,1,1,4,32,128]{5,4,3,2,0,1:T(8,128)}, u32[]{:S(2)}) copy-start(f32[16,1,1,4,32,128]{5,4,3,2,0,1:T(8,128)} %get-tuple-element.20) | copy-start | bytes 3145732
  417.8 19.5 %copy-start.6 = (f32[16,1,1,4,32,128]{5,4,3,2,0,1:T(8,128)S(1)}, f32[16,1,1,4,32,128]{5,4,3,2,0,1:T(8,128)}, u32[]{:S(2)}) copy-start(f32[16,1,1,4,32,128]{5,4,3,2,0,1:T(8,128)} %get-tuple-element.14) | copy-start | bytes 3145732
  445.9 26.1 %collective-permute-start.6 = (f32[16,4,1,1,32,128]{5,4,2,1,0,3:T(8,128)S(1)}, f32[16,4,1,1,32,128]{5,4,2,1,0,3:T(8,128)S(1)}, u32[]{:S(2)}, u32[]{:S(2)}) collective-permute-start(f32[16,4,1,1,32,128]{5,4,2,1,0,3:T(8,128)S(1)} %get-tuple-element.13), channel_id=1, source_target_pairs={{0,1},{1,0},{2,3},{3,2},{4,5},{5,4},{6,7},{7,6},{8,9},{9,8},{10,11... | collective-permute-start | bytes 3145736 | tf_op jit(solution)/shard_map/ppermute | solution.py:16
  449.9 42.8 %collective-permute-start.9 = (f32[16,4,1,1,32,128]{5,4,2,1,0,3:T(8,128)S(1)}, f32[16,4,1,1,32,128]{5,4,2,1,0,3:T(8,128)S(1)}, u32[]{:S(2)}, u32[]{:S(2)}) collective-permute-start(f32[16,4,1,1,32,128]{5,4,2,1,0,3:T(8,128)S(1)} %get-tuple-element.7), channel_id=1, source_target_pairs={{0,1},{1,0},{2,3},{3,2},{4,5},{5,4},{6,7},{7,6},{8,9},{9,8},{10,11... | collective-permute-start | bytes 3145736 | tf_op jit(solution)/shard_map/ppermute | solution.py:16
  472.5 21.7 %collective-permute-start.7 = (f32[16,2,1,2,32,128]{5,4,3,2,1,0:T(8,128)S(1)}, f32[16,2,1,2,32,128]{5,4,3,2,1,0:T(8,128)S(1)}, u32[]{:S(2)}, u32[]{:S(2)}) collective-permute-start(f32[16,2,1,2,32,128]{5,4,3,2,1,0:T(8,128)S(1)} %get-tuple-element.11), channel_id=1, source_target_pairs={{0,2},{2,0},{1,3},{3,1},{4,6},{6,4},{5,7},{7,5},{8,10},{10,8},{9,1... | collective-permute-start | bytes 3145736 | tf_op jit(solution)/shard_map/ppermute | solution.py:16
  493.1 26.1 %collective-permute-start.10 = (f32[16,2,1,2,32,128]{5,4,3,2,1,0:T(8,128)S(1)}, f32[16,2,1,2,32,128]{5,4,3,2,1,0:T(8,128)S(1)}, u32[]{:S(2)}, u32[]{:S(2)}) collective-permute-start(f32[16,2,1,2,32,128]{5,4,3,2,1,0:T(8,128)S(1)} %get-tuple-element.5), channel_id=1, source_target_pairs={{0,2},{2,0},{1,3},{3,1},{4,6},{6,4},{5,7},{7,5},{8,10},{10,8},{9,1... | collective-permute-start | bytes 3145736 | tf_op jit(solution)/shard_map/ppermute | solution.py:16
  494.6 48.2 %collective-permute-start.8 = (f32[16,1,1,4,32,128]{5,4,3,2,0,1:T(8,128)S(1)}, f32[16,1,1,4,32,128]{5,4,3,2,0,1:T(8,128)S(1)}, u32[]{:S(2)}, u32[]{:S(2)}) collective-permute-start(f32[16,1,1,4,32,128]{5,4,3,2,0,1:T(8,128)S(1)} %get-tuple-element.9), channel_id=1, source_target_pairs={{0,4},{4,0},{1,5},{5,1},{2,6},{6,2},{3,7},{7,3},{8,12},{12,8},{9,1... | collective-permute-start | bytes 3145736 | tf_op jit(solution)/shard_map/ppermute | solution.py:16
  519.7 42.7 %collective-permute-start.11 = (f32[16,1,1,4,32,128]{5,4,3,2,0,1:T(8,128)S(1)}, f32[16,1,1,4,32,128]{5,4,3,2,0,1:T(8,128)S(1)}, u32[]{:S(2)}, u32[]{:S(2)}) collective-permute-start(f32[16,1,1,4,32,128]{5,4,3,2,0,1:T(8,128)S(1)} %get-tuple-element.3), channel_id=1, source_target_pairs={{0,4},{4,0},{1,5},{5,1},{2,6},{6,2},{3,7},{7,3},{8,12},{12,8},{9,1... | collective-permute-start | bytes 3145736 | tf_op jit(solution)/shard_map/ppermute | solution.py:16
  562.4 2.3 copy-start.1
where the time goes:
time: 575 us; the launch traced here: 565 us
  waiting for transfers between devices  337 us (59%)
  starting transfers between devices  75 us (13%)
  matrix products  66.5 us (12%)
  other arithmetic  44.2 us (8%)
  local copies, waits for them, and re-layouts  41.4 us (7%)
    ppermute x12, waiting for transfers between devices, partner(): return lax.ppermute(block, axis, route)  185 us
    all_to_all x1, waiting for transfers between devices, body(): lax.all_to_all(pieces[1], 'wide', split_axis=2, concat_axis=0, tiled=True)  39.9 us
    all_to_all x1, waiting for transfers between devices, body(): lax.all_to_all(pieces[0], 'wide', split_axis=2, concat_axis=0, tiled=True)  39.6 us
    all_to_all x1, waiting for transfers between devices, body(): lax.all_to_all(pieces[1], 'wide', split_axis=0, concat_axis=2, tiled=True)  36.9 us
    all_to_all x1, waiting for transfers between devices, body(): lax.all_to_all(pieces[0], 'wide', split_axis=0, concat_axis=2, tiled=True)  34.7 us
    dot_general x1, matrix products, body(): jnp.dot(real_part, first_gate[1].T, precision=precise)  30.1 us
    add x1, other arithmetic, phase_turn(): real_part * sine + imag_part * cosine  26.3 us
    ppermute x12, starting transfers between devices, partner(): return lax.ppermute(block, axis, route)  26.2 us
  transfers between devices with their start and end apart: 16, of which 16 were waited for; matrix products, arithmetic and copies ran while one was open for 10% of the time, Pallas kernels for 0%

commit v1 on v0

--- a/solution.py
+++ b/solution.py
@@ -4,6 +4,13 @@
 from jax.sharding import PartitionSpec as P
 
 precise = lax.Precision.HIGHEST
+
+
+def stacked_exchange(array, mesh_axis, split, join):
+    size = lax.axis_size(mesh_axis)
+    pieces = jnp.stack(jnp.split(array, size, axis=split), axis=0)
+    pieces = lax.all_to_all(pieces, mesh_axis, split_axis=0, concat_axis=0)
+    return jnp.concatenate(pieces, axis=join)
 
 
 def partner(block, axis, stride):
@@ -157,7 +164,7 @@
         wide_count,
         lambda pieces: (
             lax.all_to_all(pieces[0], "wide", split_axis=2, concat_axis=0, tiled=True),
-            lax.all_to_all(pieces[1], "wide", split_axis=2, concat_axis=0, tiled=True),
+            stacked_exchange(pieces[1], "wide", 2, 0),
         ),
         lambda pieces: (
             lax.all_to_all(pieces[0], "wide", split_axis=0, concat_axis=2, tiled=True),

time: 575 us -> 550 us (0.957)
  waiting for transfers between devices: 337 us -> 302 us
  local copies, waits for them, and re-layouts: 41.4 us -> 53.7 us
  starting transfers between devices: 75 us -> 64.5 us
  matrix products: 66.5 us -> 72.3 us
    all_to_all x1, waiting for transfers between devices: 39.6 us -> 0.01 us  [body(): lax.all_to_all(pieces[0], 'wide', split_axis=2, concat_axis=0, tiled=True)]
    unnamed x20 -> x59, local copies, waits for them, and re-layouts: 5.12 us -> 24.8 us
  transfers between devices with their start and end apart: 16 -> 16, of which waited for: 16 -> 15; matrix products, arithmetic and copies ran while one was open for 10% -> 19% of each run, Pallas kernels for 0% -> 0%
where the time goes in v1:
time: 550 us; the launch traced here: 540 us
  waiting for transfers between devices  302 us (55%)
  matrix products  72.3 us (13%)
  starting transfers between devices  64.5 us (12%)
  local copies, waits for them, and re-layouts  53.7 us (10%)
  other arithmetic  46 us (8%)
    ppermute x12, waiting for transfers between devices, partner(): return lax.ppermute(block, axis, route)  186 us
    all_to_all x1, waiting for transfers between devices, stacked_exchange(): pieces = lax.all_to_all(pieces, mesh_axis, split_axis=0, concat_axis=0)  43.5 us
    all_to_all x1, waiting for transfers between devices, body(): lax.all_to_all(pieces[0], 'wide', split_axis=0, concat_axis=2, tiled=True)  39.8 us
    all_to_all x1, waiting for transfers between devices, body(): lax.all_to_all(pieces[1], 'wide', split_axis=0, concat_axis=2, tiled=True)  33.5 us
    dot_general x1, matrix products, body(): jnp.dot(real_part, first_gate[1].T, precision=precise)  30.2 us
    add x1, other arithmetic, phase_turn(): real_part * sine + imag_part * cosine  28.4 us
    unnamed x59, local copies, waits for them, and re-layouts  24.8 us
    ppermute x12, starting transfers between devices, partner(): return lax.ppermute(block, axis, route)  22.7 us
  transfers between devices with their start and end apart: 16, of which 15 were waited for; matrix products, arithmetic and copies ran while one was open for 19% of the time, Pallas kernels for 0%

profile of v1, /device:TPU:2, one launch (start us, length us, event | category | flops | bytes accessed | tf_op | source)
XLA Modules:
  0.0 540.1 jit_solution(10141467080731996586)
XLA Ops:
  4.4 3.3 fusion.18
  7.6 3.3 fusion.14
  12.3 4.3 fusion.1
  16.6 30.2 %multiply_subtract_fusion = (f32[4096,128]{0,1:T(8,128)}, f32[4096,128]{0,1:T(8,128)}) fusion(f32[4096,128]{0,1:T(8,128)S(1)} %fusion.1, f32[]{:T(128)} %bitcast.34, s32[]{:T(128)} %bitcast.33, s32[]{:T(128)} %bitcast.32, f32[]{:T(128)} %bitcast.31, s32[]{:T(128)} %bitcast.30, s32[]{:T(128)} %bitcast.29, f32[]{:T(128)} %bitcast.28, s32[]{:T(128)} %bitcast.27, ...), kind=kOutput, calls=%fused_computation.39 | convolution fusion | flops 836763648 | bytes 10567776 | tf_op jit(solution)/shard_map/dot_general | solution.py:145
  52.1 11.8 %all-to-all-start = ((f32[1,4,1024,128]{3,1,0,2:T(4,128)}), f32[1,4,1024,128]{3,1,0,2:T(4,128)}, u32[]{:S(2)}, u32[]{:S(2)}) async-start(f32[1,4,1024,128]{3,1,0,2:T(4,128)} %copy.132), calls=%async_computation | async-start | bytes 4194304 | tf_op jit(solution)/shard_map/all_to_all | solution.py:166
  63.9 28.4 %multiply_add_fusion = f32[4096,128]{0,1:T(8,128)} fusion(f32[4096,128]{0,1:T(8,128)} %get-tuple-element.54, f32[4096,128]{0,1:T(8,128)S(1)} %copy-done.5, f32[]{:T(128)} %bitcast.34, s32[]{:T(128)} %bitcast.33, s32[]{:T(128)} %bitcast.32, f32[]{:T(128)} %bitcast.31, s32[]{:T(128)} %bitcast.30, s32[]{:T(128)} %bitcast.29, f32[]{:T(128)} %bitcast.28, ...), kind=kLoop, calls=%fused_computation.38 | loop fusion | flops 30932992 | bytes 6307936 | tf_op jit(solution)/shard_map/add | solution.py:59
  114.5 10.2 %all-to-all-start.1 = ((f32[32,1,4,32,128]{4,3,2,1,0:T(8,128)}), f32[32,1,4,32,128]{4,3,2,1,0:T(8,128)S(1)}, u32[]{:S(2)}, u32[]{:S(2)}) async-start(f32[32,1,4,32,128]{4,3,2,1,0:T(8,128)} %constant_dynamic-update-slice_fusion), calls=%async_computation.1 | async-start | bytes 4194304 | tf_op jit(solution)/shard_map/all_to_all | solution.py:12
  129.1 43.5 %all-to-all-done.1 = f32[32,1,4,32,128]{4,3,2,1,0:T(8,128)S(1)} async-done(((f32[32,1,4,32,128]{4,3,2,1,0:T(8,128)}), f32[32,1,4,32,128]{4,3,2,1,0:T(8,128)S(1)}, u32[]{:S(2)}, u32[]{:S(2)}) %all-to-all-start.1) | async-done | bytes 2097184 | tf_op jit(solution)/shard_map/all_to_all | solution.py:12
  175.6 3.0 fusion.39
  180.4 9.0 %all-to-all-start.3 = ((f32[32,4,32,128]{3,2,1,0:T(8,128)}), f32[32,4,32,128]{3,2,1,0:T(8,128)}, u32[]{:S(2)}, u32[]{:S(2)}) async-start(f32[32,4,32,128]{3,2,1,0:T(8,128)} %bitcast.354), calls=%async_computation.3 | async-start | bytes 4194304 | tf_op jit(solution)/shard_map/all_to_all | solution.py:171
  189.3 4.6 fusion.12
  193.9 3.0 fusion.36
  198.6 33.5 %all-to-all-done.3 = f32[32,4,32,128]{3,2,1,0:T(8,128)} async-done(((f32[32,4,32,128]{3,2,1,0:T(8,128)}), f32[32,4,32,128]{3,2,1,0:T(8,128)}, u32[]{:S(2)}, u32[]{:S(2)}) %all-to-all-start.3) | async-done | bytes 2097184 | tf_op jit(solution)/shard_map/all_to_all | solution.py:171
  232.1 10.8 %all-to-all-start.2 = ((f32[32,4,32,128]{3,2,1,0:T(8,128)}), f32[32,4,32,128]{3,2,1,0:T(8,128)}, u32[]{:S(2)}, u32[]{:S(2)}) async-start(f32[32,4,32,128]{3,2,1,0:T(8,128)} %bitcast.113), calls=%async_computation.2 | async-start | bytes 4194304 | tf_op jit(solution)/shard_map/all_to_all | solution.py:170
  246.3 4.3 collective-permute-start.3
  250.6 39.8 %all-to-all-done.2 = f32[32,4,32,128]{3,2,1,0:T(8,128)} async-done(((f32[32,4,32,128]{3,2,1,0:T(8,128)}), f32[32,4,32,128]{3,2,1,0:T(8,128)}, u32[]{:S(2)}, u32[]{:S(2)}) %all-to-all-start.2) | async-done | bytes 2097184 | tf_op jit(solution)/shard_map/all_to_all | solution.py:170
  293.4 4.2 collective-permute-start
  297.6 16.2 %collective-permute-done.3 = f32[16,4,1,1,32,128]{5,4,2,1,0,3:T(8,128)} collective-permute-done((f32[16,4,1,1,32,128]{5,4,2,1,0,3:T(8,128)}, f32[16,4,1,1,32,128]{5,4,2,1,0,3:T(8,128)}, u32[]{:S(2)}, u32[]{:S(2)}) %collective-permute-start.3) | collective-permute-done | bytes 1048608 | tf_op jit(solution)/shard_map/ppermute | solution.py:23
  319.9 16.4 %collective-permute-done = f32[16,4,1,1,32,128]{5,4,2,1,0,3:T(8,128)} collective-permute-done((f32[16,4,1,1,32,128]{5,4,2,1,0,3:T(8,128)}, f32[16,4,1,1,32,128]{5,4,2,1,0,3:T(8,128)}, u32[]{:S(2)}, u32[]{:S(2)}) %collective-permute-start) | collective-permute-done | bytes 1048608 | tf_op jit(solution)/shard_map/ppermute | solution.py:23
  341.0 3.7 collective-permute-done.4
  349.1 3.6 collective-permute-start.5
  352.9 14.2 %collective-permute-done.1 = f32[16,2,1,2,32,128]{5,4,3,2,1,0:T(8,128)} collective-permute-done((f32[16,2,1,2,32,128]{5,4,3,2,1,0:T(8,128)}, f32[16,2,1,2,32,128]{5,4,3,2,1,0:T(8,128)}, u32[]{:S(2)}, u32[]{:S(2)}) %collective-permute-start.1) | collective-permute-done | bytes 1048608 | tf_op jit(solution)/shard_map/ppermute | solution.py:23
  370.7 3.2 collective-permute-start.2
  377.7 14.3 %collective-permute-done.5 = f32[16,1,1,4,32,128]{5,4,3,2,0,1:T(8,128)} collective-permute-done((f32[16,1,1,4,32,128]{5,4,3,2,0,1:T(8,128)}, f32[16,1,1,4,32,128]{5,4,3,2,0,1:T(8,128)}, u32[]{:S(2)}, u32[]{:S(2)}) %collective-permute-start.5) | collective-permute-done | bytes 1048608 | tf_op jit(solution)/shard_map/ppermute | solution.py:23
  397.0 16.5 %collective-permute-done.2 = f32[16,1,1,4,32,128]{5,4,3,2,0,1:T(8,128)} collective-permute-done((f32[16,1,1,4,32,128]{5,4,3,2,0,1:T(8,128)}, f32[16,1,1,4,32,128]{5,4,3,2,0,1:T(8,128)}, u32[]{:S(2)}, u32[]{:S(2)}) %collective-permute-start.2) | collective-permute-done | bytes 1048608 | tf_op jit(solution)/shard_map/ppermute | solution.py:23
  418.5 3.0 fusion.45
  422.4 3.0 fusion.42
  428.1 20.3 %collective-permute-done.9 = f32[16,4,1,1,32,128]{5,4,2,1,0,3:T(8,128)S(1)} collective-permute-done((f32[16,4,1,1,32,128]{5,4,2,1,0,3:T(8,128)S(1)}, f32[16,4,1,1,32,128]{5,4,2,1,0,3:T(8,128)S(1)}, u32[]{:S(2)}, u32[]{:S(2)}) %collective-permute-start.9) | collective-permute-done | bytes 1048608 | tf_op jit(solution)/shard_map/ppermute | solution.py:23
  449.1 20.0 %collective-permute-done.6 = f32[16,4,1,1,32,128]{5,4,2,1,0,3:T(8,128)S(1)} collective-permute-done((f32[16,4,1,1,32,128]{5,4,2,1,0,3:T(8,128)S(1)}, f32[16,4,1,1,32,128]{5,4,2,1,0,3:T(8,128)S(1)}, u32[]{:S(2)}, u32[]{:S(2)}) %collective-permute-start.6) | collective-permute-done | bytes 1048608 | tf_op jit(solution)/shard_map/ppermute | solution.py:23
  471.8 23.8 %collective-permute-done.7 = f32[16,2,1,2,32,128]{5,4,3,2,1,0:T(8,128)S(1)} collective-permute-done((f32[16,2,1,2,32,128]{5,4,3,2,1,0:T(8,128)S(1)}, f32[16,2,1,2,32,128]{5,4,3,2,1,0:T(8,128)S(1)}, u32[]{:S(2)}, u32[]{:S(2)}) %collective-permute-start.7) | collective-permute-done | bytes 1048608 | tf_op jit(solution)/shard_map/ppermute | solution.py:23
  496.8 21.0 %collective-permute-done.11 = f32[16,1,1,4,32,128]{5,4,3,2,0,1:T(8,128)S(1)} collective-permute-done((f32[16,1,1,4,32,128]{5,4,3,2,0,1:T(8,128)S(1)}, f32[16,1,1,4,32,128]{5,4,3,2,0,1:T(8,128)S(1)}, u32[]{:S(2)}, u32[]{:S(2)}) %collective-permute-start.11) | collective-permute-done | bytes 1048608 | tf_op jit(solution)/shard_map/ppermute | solution.py:23
  519.3 18.3 %collective-permute-done.8 = f32[16,1,1,4,32,128]{5,4,3,2,0,1:T(8,128)S(1)} collective-permute-done((f32[16,1,1,4,32,128]{5,4,3,2,0,1:T(8,128)S(1)}, f32[16,1,1,4,32,128]{5,4,3,2,0,1:T(8,128)S(1)}, u32[]{:S(2)}, u32[]{:S(2)}) %collective-permute-start.8) | collective-permute-done | bytes 1048608 | tf_op jit(solution)/shard_map/ppermute | solution.py:23
  (128 shorter events, 94.0 us)
Async XLA Ops:
  0.6 3.7 copy-start
  4.3 3.3 copy-start.3
  7.6 3.3 copy-start.10
  7.6 4.0 copy-start.11
  12.3 4.3 copy-start.8
  16.6 30.2 %copy-start.4 = (f32[4096,128]{0,1:T(8,128)}, f32[4096,128]{0,1:T(8,128)S(1)}, u32[]{:S(2)}) copy-start(f32[4096,128]{0,1:T(8,128)S(1)} %fusion.1) | copy-start | bytes 6291460
  52.1 11.8 %copy-start.5 = (f32[4096,128]{0,1:T(8,128)S(1)}, f32[4096,128]{0,1:T(8,128)}, u32[]{:S(2)}) copy-start(f32[4096,128]{0,1:T(8,128)} %copy-done.4) | copy-start | bytes 6291460
  52.1 62.4 %all-to-all-start = ((f32[1,4,1024,128]{3,1,0,2:T(4,128)}), f32[1,4,1024,128]{3,1,0,2:T(4,128)}, u32[]{:S(2)}, u32[]{:S(2)}) async-start(f32[1,4,1024,128]{3,1,0,2:T(4,128)} %copy.132), calls=%async_computation | async-start | bytes 4194304 | tf_op jit(solution)/shard_map/all_to_all | solution.py:166
  114.5 10.3 %copy-start.9 = (f32[3,2,128,128]{3,2,1,0:T(8,128)S(1)}, f32[3,2,128,128]{3,2,1,0:T(8,128)}, u32[]{:S(2)}) copy-start(f32[3,2,128,128]{3,2,1,0:T(8,128)} %param.8) | copy-start | bytes 1179652
  114.5 58.1 %all-to-all-start.1 = ((f32[32,1,4,32,128]{4,3,2,1,0:T(8,128)}), f32[32,1,4,32,128]{4,3,2,1,0:T(8,128)S(1)}, u32[]{:S(2)}, u32[]{:S(2)}) async-start(f32[32,1,4,32,128]{4,3,2,1,0:T(8,128)} %constant_dynamic-update-slice_fusion), calls=%async_computation.1 | async-start | bytes 4194304 | tf_op jit(solution)/shard_map/all_to_all | solution.py:12
  172.6 3.0 copy-start.2
  180.4 51.7 %all-to-all-start.3 = ((f32[32,4,32,128]{3,2,1,0:T(8,128)}), f32[32,4,32,128]{3,2,1,0:T(8,128)}, u32[]{:S(2)}, u32[]{:S(2)}) async-start(f32[32,4,32,128]{3,2,1,0:T(8,128)} %bitcast.354), calls=%async_computation.3 | async-start | bytes 4194304 | tf_op jit(solution)/shard_map/all_to_all | solution.py:171
  232.1 58.3 %all-to-all-start.2 = ((f32[32,4,32,128]{3,2,1,0:T(8,128)}), f32[32,4,32,128]{3,2,1,0:T(8,128)}, u32[]{:S(2)}, u32[]{:S(2)}) async-start(f32[32,4,32,128]{3,2,1,0:T(8,128)} %bitcast.113), calls=%async_computation.2 | async-start | bytes 4194304 | tf_op jit(solution)/shard_map/all_to_all | solution.py:170
  246.3 67.5 %collective-permute-start.3 = (f32[16,4,1,1,32,128]{5,4,2,1,0,3:T(8,128)}, f32[16,4,1,1,32,128]{5,4,2,1,0,3:T(8,128)}, u32[]{:S(2)}, u32[]{:S(2)}) collective-permute-start(f32[16,4,1,1,32,128]{5,4,2,1,0,3:T(8,128)} %get-tuple-element.19), channel_id=1, source_target_pairs={{0,1},{1,0},{2,3},{3,2},{4,5},{5,4},{6,7},{7,6},{8,9},{9,8},{10,11... | collective-permute-start | bytes 3145736 | tf_op jit(solution)/shard_map/ppermute | solution.py:23
  293.4 42.9 %collective-permute-start = (f32[16,4,1,1,32,128]{5,4,2,1,0,3:T(8,128)}, f32[16,4,1,1,32,128]{5,4,2,1,0,3:T(8,128)}, u32[]{:S(2)}, u32[]{:S(2)}) collective-permute-start(f32[16,4,1,1,32,128]{5,4,2,1,0,3:T(8,128)} %get-tuple-element.25), channel_id=1, source_target_pairs={{0,1},{1,0},{2,3},{3,2},{4,5},{5,4},{6,7},{7,6},{8,9},{9,8},{10,11... | collective-permute-start | bytes 3145736 | tf_op jit(solution)/shard_map/ppermute | solution.py:23
  318.3 26.3 %collective-permute-start.4 = (f32[16,2,1,2,32,128]{5,4,3,2,1,0:T(8,128)}, f32[16,2,1,2,32,128]{5,4,3,2,1,0:T(8,128)}, u32[]{:S(2)}, u32[]{:S(2)}) collective-permute-start(f32[16,2,1,2,32,128]{5,4,3,2,1,0:T(8,128)} %get-tuple-element.17), channel_id=1, source_target_pairs={{0,2},{2,0},{1,3},{3,1},{4,6},{6,4},{5,7},{7,5},{8,10},{10,8},{9,1... | collective-permute-start | bytes 3145736 | tf_op jit(solution)/shard_map/ppermute | solution.py:23
  339.4 27.7 %collective-permute-start.1 = (f32[16,2,1,2,32,128]{5,4,3,2,1,0:T(8,128)}, f32[16,2,1,2,32,128]{5,4,3,2,1,0:T(8,128)}, u32[]{:S(2)}, u32[]{:S(2)}) collective-permute-start(f32[16,2,1,2,32,128]{5,4,3,2,1,0:T(8,128)} %get-tuple-element.23), channel_id=1, source_target_pairs={{0,2},{2,0},{1,3},{3,1},{4,6},{6,4},{5,7},{7,5},{8,10},{10,8},{9,1... | collective-permute-start | bytes 3145736 | tf_op jit(solution)/shard_map/ppermute | solution.py:23
  349.1 43.0 %collective-permute-start.5 = (f32[16,1,1,4,32,128]{5,4,3,2,0,1:T(8,128)}, f32[16,1,1,4,32,128]{5,4,3,2,0,1:T(8,128)}, u32[]{:S(2)}, u32[]{:S(2)}) collective-permute-start(f32[16,1,1,4,32,128]{5,4,3,2,0,1:T(8,128)} %get-tuple-element.15), channel_id=1, source_target_pairs={{0,4},{4,0},{1,5},{5,1},{2,6},{6,2},{3,7},{7,3},{8,12},{12,8},{9,1... | collective-permute-start | bytes 3145736 | tf_op jit(solution)/shard_map/ppermute | solution.py:23
  370.7 42.8 %collective-permute-start.2 = (f32[16,1,1,4,32,128]{5,4,3,2,0,1:T(8,128)}, f32[16,1,1,4,32,128]{5,4,3,2,0,1:T(8,128)}, u32[]{:S(2)}, u32[]{:S(2)}) collective-permute-start(f32[16,1,1,4,32,128]{5,4,3,2,0,1:T(8,128)} %get-tuple-element.21), channel_id=1, source_target_pairs={{0,4},{4,0},{1,5},{5,1},{2,6},{6,2},{3,7},{7,3},{8,12},{12,8},{9,1... | collective-permute-start | bytes 3145736 | tf_op jit(solution)/shard_map/ppermute | solution.py:23
  374.8 17.3 %copy-start.6 = (f32[16,1,1,4,32,128]{5,4,3,2,0,1:T(8,128)S(1)}, f32[16,1,1,4,32,128]{5,4,3,2,0,1:T(8,128)}, u32[]{:S(2)}) copy-start(f32[16,1,1,4,32,128]{5,4,3,2,0,1:T(8,128)} %get-tuple-element.14) | copy-start | bytes 3145732
  394.0 19.6 %copy-start.7 = (f32[16,1,1,4,32,128]{5,4,3,2,0,1:T(8,128)S(1)}, f32[16,1,1,4,32,128]{5,4,3,2,0,1:T(8,128)}, u32[]{:S(2)}) copy-start(f32[16,1,1,4,32,128]{5,4,3,2,0,1:T(8,128)} %get-tuple-element.20) | copy-start | bytes 3145732
  422.3 26.1 %collective-permute-start.9 = (f32[16,4,1,1,32,128]{5,4,2,1,0,3:T(8,128)S(1)}, f32[16,4,1,1,32,128]{5,4,2,1,0,3:T(8,128)S(1)}, u32[]{:S(2)}, u32[]{:S(2)}) collective-permute-start(f32[16,4,1,1,32,128]{5,4,2,1,0,3:T(8,128)S(1)} %get-tuple-element.7), channel_id=1, source_target_pairs={{0,1},{1,0},{2,3},{3,2},{4,5},{5,4},{6,7},{7,6},{8,9},{9,8},{10,11... | collective-permute-start | bytes 3145736 | tf_op jit(solution)/shard_map/ppermute | solution.py:23
  426.0 43.1 %collective-permute-start.6 = (f32[16,4,1,1,32,128]{5,4,2,1,0,3:T(8,128)S(1)}, f32[16,4,1,1,32,128]{5,4,2,1,0,3:T(8,128)S(1)}, u32[]{:S(2)}, u32[]{:S(2)}) collective-permute-start(f32[16,4,1,1,32,128]{5,4,2,1,0,3:T(8,128)S(1)} %get-tuple-element.13), channel_id=1, source_target_pairs={{0,1},{1,0},{2,3},{3,2},{4,5},{5,4},{6,7},{7,6},{8,9},{9,8},{10,11... | collective-permute-start | bytes 3145736 | tf_op jit(solution)/shard_map/ppermute | solution.py:23
  448.8 21.6 %collective-permute-start.10 = (f32[16,2,1,2,32,128]{5,4,3,2,1,0:T(8,128)S(1)}, f32[16,2,1,2,32,128]{5,4,3,2,1,0:T(8,128)S(1)}, u32[]{:S(2)}, u32[]{:S(2)}) collective-permute-start(f32[16,2,1,2,32,128]{5,4,3,2,1,0:T(8,128)S(1)} %get-tuple-element.5), channel_id=1, source_target_pairs={{0,2},{2,0},{1,3},{3,1},{4,6},{6,4},{5,7},{7,5},{8,10},{10,8},{9,1... | collective-permute-start | bytes 3145736 | tf_op jit(solution)/shard_map/ppermute | solution.py:23
  469.5 26.1 %collective-permute-start.7 = (f32[16,2,1,2,32,128]{5,4,3,2,1,0:T(8,128)S(1)}, f32[16,2,1,2,32,128]{5,4,3,2,1,0:T(8,128)S(1)}, u32[]{:S(2)}, u32[]{:S(2)}) collective-permute-start(f32[16,2,1,2,32,128]{5,4,3,2,1,0:T(8,128)S(1)} %get-tuple-element.11), channel_id=1, source_target_pairs={{0,2},{2,0},{1,3},{3,1},{4,6},{6,4},{5,7},{7,5},{8,10},{10,8},{9,1... | collective-permute-start | bytes 3145736 | tf_op jit(solution)/shard_map/ppermute | solution.py:23
  470.9 46.8 %collective-permute-start.11 = (f32[16,1,1,4,32,128]{5,4,3,2,0,1:T(8,128)S(1)}, f32[16,1,1,4,32,128]{5,4,3,2,0,1:T(8,128)S(1)}, u32[]{:S(2)}, u32[]{:S(2)}) collective-permute-start(f32[16,1,1,4,32,128]{5,4,3,2,0,1:T(8,128)S(1)} %get-tuple-element.3), channel_id=1, source_target_pairs={{0,4},{4,0},{1,5},{5,1},{2,6},{6,2},{3,7},{7,3},{8,12},{12,8},{9,1... | collective-permute-start | bytes 3145736 | tf_op jit(solution)/shard_map/ppermute | solution.py:23
  496.0 41.5 %collective-permute-start.8 = (f32[16,1,1,4,32,128]{5,4,3,2,0,1:T(8,128)S(1)}, f32[16,1,1,4,32,128]{5,4,3,2,0,1:T(8,128)S(1)}, u32[]{:S(2)}, u32[]{:S(2)}) collective-permute-start(f32[16,1,1,4,32,128]{5,4,3,2,0,1:T(8,128)S(1)} %get-tuple-element.9), channel_id=1, source_target_pairs={{0,4},{4,0},{1,5},{5,1},{2,6},{6,2},{3,7},{7,3},{8,12},{12,8},{9,1... | collective-permute-start | bytes 3145736 | tf_op jit(solution)/shard_map/ppermute | solution.py:23
  537.5 2.3 copy-start.1
